TPU v7x, 256 devices: a whole 4x4x8 slice. The times are simulated.
256 devices in a mesh: dp: 32 (over z_hi, x, core), tensor: 8 (over z_lo, y).
Axes of the slice: x: 4, y: 4, z: 8 (z_hi: 4, z_lo: 2; z = z_hi * 2 + z_lo), core: 2. Of those that a mesh axis runs over, the one named last changes fastest.
Arguments:
- quant_rows: int32 [32768, 2048], P(('dp', 'tensor')), may hold values from -127 to 127
- residual: bfloat16 [32768, 2048], P(('dp', 'tensor')), may hold values from -48 to 48
- row_scale: float32 [32768], P(('dp', 'tensor')), may hold values from 0.004 to 0.04
- norm_gain: float32 [2048], replicated, may hold values from 0.1 to 1.9
- gate_pre: bfloat16 [32768, 7168], P('dp', 'tensor'), may hold values from -6 to 6
- up_pre: bfloat16 [32768, 7168], P('dp', 'tensor'), may hold values from -6 to 6
- hidden_grad: bfloat16 [32768, 7168], P('dp', 'tensor'), may hold values from -6 to 6
- gate_weight: bfloat16 [2048, 7168], P('dp', 'tensor'), may hold values from -0.125 to 0.125
- up_weight: bfloat16 [2048, 7168], P('dp', 'tensor'), may hold values from -0.125 to 0.125
Outputs:
- resid_grad: bfloat16 [32768, 2048], P(('dp', 'tensor'))
- gate_weight_grad: float32 [2048, 7168], P('dp', 'tensor')
- up_weight_grad: float32 [2048, 7168], P('dp', 'tensor')
All inputs are finite; a program needn't handle non-finite values.
Results may differ from a plain program's by a relative error of at most 0.014.
Values may be sent and summed in bfloat16 or wider, within the bound.
No kernel may reach another device: no remote copies, remote signals or barrier semaphores. Data moves between devices by JAX's collectives and lax.ppermute only.
A program may use at most 64 MiB of HBM per device.

v0:
```python
import math
import jax
import jax.numpy as jnp
from jax import lax
from jax.sharding import PartitionSpec as P


def body(
    quant_rows,
    residual,
    row_scale,
    norm_gain,
    gate_pre,
    up_pre,
    hidden_grad,
    gate_weight,
    up_weight,
):
    summed_in = residual.astype(jnp.float32) + quant_rows.astype(jnp.float32) * row_scale[:, None]
    inverse = lax.rsqrt(jnp.mean(summed_in * summed_in, axis=-1, keepdims=True) + 1e-05)
    unit_rows = summed_in * inverse
    normed = (unit_rows * norm_gain).astype(jnp.bfloat16)
    gathered = lax.all_gather(normed, "tensor", axis=0, tiled=True)
    gate_val = gate_pre.astype(jnp.float32)
    up_val = up_pre.astype(jnp.float32)
    grad_val = hidden_grad.astype(jnp.float32)
    sigmoid_gate = jax.nn.sigmoid(gate_val)
    up_grad = (grad_val * gate_val * sigmoid_gate).astype(jnp.bfloat16)
    gate_grad = (grad_val * up_val * sigmoid_gate * (1.0 + gate_val * (1.0 - sigmoid_gate))).astype(
        jnp.bfloat16
    )
    grad_cat = jnp.concatenate((gate_grad, up_grad), axis=1)
    weight_cat = jnp.concatenate((gate_weight, up_weight), axis=1)
    partial_value = jnp.einsum(
        "rf,nf->rn",
        grad_cat,
        lax.all_gather(weight_cat, "dp", axis=0, tiled=True),
        preferred_element_type=jnp.float32,
    )
    normed_grad = lax.psum_scatter(
        partial_value.astype(jnp.bfloat16), "tensor", scatter_dimension=0, tiled=True
    ).astype(jnp.float32)
    grad_term = norm_gain * normed_grad
    input_grad = inverse * (
        grad_term - unit_rows * jnp.mean(unit_rows * grad_term, axis=-1, keepdims=True)
    )
    resid_grad = input_grad.astype(jnp.bfloat16)
    tokens_all = gate_pre.shape[0] * lax.axis_size("dp")
    factor = 1.0 / math.sqrt(tokens_all)
    weight_part = lax.dot_general(
        gathered, grad_cat, (((0,), (0,)), ((), ())), preferred_element_type=jnp.float32
    )
    own_rows = lax.psum_scatter(
        weight_part.astype(jnp.bfloat16), "dp", scatter_dimension=0, tiled=True
    ).astype(jnp.float32)
    scaled_grad = own_rows * factor
    hidden_width = gate_weight.shape[1]
    return (resid_grad, scaled_grad[:, :hidden_width], scaled_grad[:, hidden_width:])


def solution(mesh):
    placed = (
        P(("dp", "tensor"), None),
        P(("dp", "tensor"), None),
        P(("dp", "tensor")),
        P(),
        P("dp", "tensor"),
        P("dp", "tensor"),
        P("dp", "tensor"),
        P("dp", "tensor"),
        P("dp", "tensor"),
    )
    return jax.shard_map(
        body,
        mesh=mesh,
        in_specs=placed,
        out_specs=(P(("dp", "tensor"), None), P("dp", "tensor"), P("dp", "tensor")),
        check_vma=False,
    )
```

profile of v0, /device:TPU:8, one launch (start us, length us, event | category | flops | bytes accessed | tf_op | source)
XLA Modules:
  0.0 346.1 jit_solution(7484512502405937982)
XLA Ops:
  7.2 0.0 all-gather.3.cloned.1.call-start
  7.2 1.7 pad_maximum_fusion.3
  8.9 0.0 all-gather.3.cloned.1.call-update
  8.9 0.0 reduce-scatter.3.cloned.1.call-start
  8.9 4.7 %fusion.2 = (bf16[1024,896]{1,0:T(8,128)(2,1)S(1)}, bf16[1024,896]{1,0:T(8,128)(2,1)}) fusion(bf16[1024,896]{1,0:T(8,128)(2,1)} %param.15, bf16[1024,896]{1,0:T(8,128)(2,1)} %param.13, bf16[1024,896]{1,0:T(8,128)(2,1)} %param.14), kind=kLoop, calls=%fused_computation.8 | loop fusion | flops 14680064 | bytes 9175040 | tf_op jit(solution)/shard_map/convert_element_type | solution.py:29
  13.6 72.9 %all-gather.3.cloned.1.call-done = bf16[2048,1792]{1,0:T(8,128)(2,1)} async-done(((bf16[64,1792]{1,0:T(8,128)(2,1)}), bf16[2048,1792]{1,0:T(8,128)(2,1)}) %all-gather.3.cloned.1.call-update) | async-done | bytes 7340048 | tf_op jit(solution)/shard_map/all_gather | solution.py:37
  86.5 12.0 %convolution_convert_fusion.1 = bf16[1024,2048]{1,0:T(8,128)(2,1)} fusion(bf16[2048,1792]{1,0:T(8,128)(2,1)} %all-gather.3.cloned.1.call-done, bf16[1024,896]{1,0:T(8,128)(2,1)} %get-tuple-element.4, bf16[1024,896]{1,0:T(8,128)(2,1)S(1)} %get-tuple-element.3), kind=kOutput, calls=%fused_computation.5 | convolution fusion | flops 7525629952 | bytes 15204352 | tf_op jit(solution)/shard_map/rf,nf->rn/dot_general | solution.py:34
  98.5 0.0 copy-start
  98.5 0.0 copy-start.1
  98.5 0.0 copy-start.3
  98.5 0.0 copy-start.2
  98.5 0.0 reduce-scatter.3.cloned.1.call-update
  98.5 0.0 all-gather.5.cloned.1.call-start
  98.6 1.1 copy-done
  99.7 0.1 copy-done.1
  99.8 0.0 copy-done.3
  99.8 0.3 multiply_reduce_fusion.1
  100.2 51.9 %reduce-scatter.3.cloned.1.call-done = bf16[128,2048]{1,0:T(8,128)(2,1)} async-done(((bf16[1024,2048]{1,0:T(8,128)(2,1)}), bf16[128,2048]{1,0:T(8,128)(2,1)}) %reduce-scatter.3.cloned.1.call-update) | async-done | bytes 524304 | tf_op jit(solution)/shard_map/reduce_scatter | solution.py:40
  152.1 0.0 copy-done.2
  152.1 1.5 multiply_reduce_fusion
  153.6 2.5 multiply_convert_fusion
  156.1 0.0 all-gather.5.cloned.1.call-update
  156.2 0.0 reduce-scatter.5.cloned.1.call-start
  156.2 53.9 %all-gather.5.cloned.1.call-done = bf16[1024,2048]{1,0:T(8,128)(2,1)} async-done(((bf16[128,2048]{1,0:T(8,128)(2,1)}), bf16[1024,2048]{1,0:T(8,128)(2,1)}) %all-gather.5.cloned.1.call-update) | async-done | bytes 4194320 | tf_op jit(solution)/shard_map/all_gather | solution.py:23
  210.1 12.1 %convolution_convert_fusion = bf16[2048,1792]{1,0:T(8,128)(2,1)} fusion(bf16[1024,2048]{1,0:T(8,128)(2,1)} %all-gather.5.cloned.1.call-done, bf16[1024,896]{1,0:T(8,128)(2,1)} %get-tuple-element.4, bf16[1024,896]{1,0:T(8,128)(2,1)S(1)} %get-tuple-element.3), kind=kOutput, calls=%fused_computation | convolution fusion | flops 7527202816 | bytes 15204352 | tf_op jit(solution)/shard_map/dot_general | solution.py:50
  222.2 0.0 reduce-scatter.5.cloned.1.call-update
  222.2 115.6 %reduce-scatter.5.cloned.1.call-done = bf16[64,1792]{1,0:T(8,128)(2,1)} async-done(((bf16[2048,1792]{1,0:T(8,128)(2,1)}), bf16[64,1792]{1,0:T(8,128)(2,1)}) %reduce-scatter.5.cloned.1.call-update) | async-done | bytes 229392 | tf_op jit(solution)/shard_map/reduce_scatter | solution.py:53
  337.8 1.0 convert_multiply_fusion.4
  338.8 0.8 fusion.11
  (2 shorter events, 0.0 us)
Async XLA Ops:
  7.2 79.3 %all-gather.3.cloned.1.call-start = ((), (), s32[]{:S(2)}) async-start(), calls=%async_computation.2 | async-start | bytes 7569408 | tf_op jit(solution)/shard_map/all_gather | solution.py:37
  8.9 143.2 %reduce-scatter.3.cloned.1.call-start = ((), (), s32[]{:S(2)}) async-start(), calls=%async_computation.3 | async-start | bytes 4718592 | tf_op jit(solution)/shard_map/reduce_scatter | solution.py:40
  98.5 1.2 copy-start
  98.5 1.4 copy-start.1
  98.5 1.4 copy-start.3
  98.5 53.6 %copy-start.2 = (f32[2048]{0:T(1024)S(1)}, f32[2048]{0:T(1024)}, u32[]{:S(2)}) copy-start(f32[2048]{0:T(1024)} %param.12) | copy-start | bytes 24580
  98.5 111.6 %all-gather.5.cloned.1.call-start = ((), (), s32[]{:S(2)}) async-start(), calls=%async_computation.4 | async-start | bytes 4718592 | tf_op jit(solution)/shard_map/all_gather | solution.py:23
  156.2 181.6 %reduce-scatter.5.cloned.1.call-start = ((), (), s32[]{:S(2)}) async-start(), calls=%async_computation.5 | async-start | bytes 7569408 | tf_op jit(solution)/shard_map/reduce_scatter | solution.py:53
Sparse Core Ops, SparseCore 0:
  11.1 75.3 all-gather.2
  98.6 53.4 reduce-scatter.2
  156.3 53.8 all-gather.4
  222.3 115.4 reduce-scatter.4
where the time goes:
time: 346 us
  waiting for transfers between devices  294 us (85%)
  matrix products  24.1 us (7%)
  between operations  13.8 us (4%)
  other arithmetic  11.7 us (3%)
    reduce_scatter x1, waiting for transfers between devices, body(): lax.psum_scatter(weight_part.astype(jnp.bfloat16), 'dp', scatter_dimensio...  116 us
    all_gather x1, waiting for transfers between devices, body(): lax.all_gather(weight_cat, 'dp', axis=0, tiled=True)  72.9 us
    all_gather x1, waiting for transfers between devices, body(): gathered = lax.all_gather(normed, 'tensor', axis=0, tiled=True)  53.9 us
    reduce_scatter x1, waiting for transfers between devices, body(): lax.psum_scatter(partial_value.astype(jnp.bfloat16), 'tensor', scatter_di...  51.9 us
    dot_general x1, matrix products, body(): lax.dot_general(gathered, grad_cat, (((0,), (0,)), ((), ())), preferred_e...  12.1 us
    dot_general x1, matrix products, body(): jnp.einsum('rf,nf->rn', grad_cat, lax.all_gather(weight_cat, 'dp', axis=0...  12 us
  transfers between devices with their start and end apart: 4, of which 4 were waited for; matrix products, arithmetic and copies ran while one was open for 1% of the time, Pallas kernels for 0%

commit v1 on v0

--- a/solution.py
+++ b/solution.py
@@ -16,6 +16,19 @@
     gate_weight,
     up_weight,
 ):
+
+    def cubes_serve(here_x):
+        v_now = jnp.concatenate(
+            jax.lax.all_to_all(
+                jnp.stack([here_x for _ in range(jax.lax.psum(1, "dp"))]),
+                axis_name="dp",
+                concat_axis=0,
+                split_axis=0,
+            ),
+            axis=0,
+        )
+        return v_now
+
     summed_in = residual.astype(jnp.float32) + quant_rows.astype(jnp.float32) * row_scale[:, None]
     inverse = lax.rsqrt(jnp.mean(summed_in * summed_in, axis=-1, keepdims=True) + 1e-05)
     unit_rows = summed_in * inverse
@@ -32,10 +45,7 @@
     grad_cat = jnp.concatenate((gate_grad, up_grad), axis=1)
     weight_cat = jnp.concatenate((gate_weight, up_weight), axis=1)
     partial_value = jnp.einsum(
-        "rf,nf->rn",
-        grad_cat,
-        lax.all_gather(weight_cat, "dp", axis=0, tiled=True),
-        preferred_element_type=jnp.float32,
+        "rf,nf->rn", grad_cat, cubes_serve(weight_cat), preferred_element_type=jnp.float32
     )
     normed_grad = lax.psum_scatter(
         partial_value.astype(jnp.bfloat16), "tensor", scatter_dimension=0, tiled=True

time: 346 us -> 444 us (1.28)
  waiting for transfers between devices: 294 us -> 377 us
  starting transfers between devices: 0.16 us -> 11.7 us
    all_to_all x0 -> x1, waiting for transfers between devices: none -> 159 us  [cubes_serve(): jax.lax.all_to_all(jnp.stack([here_x for _ in range(jax.lax.psum(1, 'dp')...]
    all_gather x1 -> x0, waiting for transfers between devices: 72.9 us -> none  [body(): lax.all_gather(weight_cat, 'dp', axis=0, tiled=True)]
    all_to_all x0 -> x1, starting transfers between devices: none -> 11.6 us  [cubes_serve(): jax.lax.all_to_all(jnp.stack([here_x for _ in range(jax.lax.psum(1, 'dp')...]
where the time goes in v1:
time: 444 us
  waiting for transfers between devices  377 us (85%)
  matrix products  24.5 us (6%)
  between operations  13.8 us (3%)
  starting transfers between devices  11.7 us (3%)
  other arithmetic  11 us (2%)
  local copies, waits for them, and re-layouts  5.91 us (1%)
    all_to_all x1, waiting for transfers between devices, cubes_serve(): jax.lax.all_to_all(jnp.stack([here_x for _ in range(jax.lax.psum(1, 'dp')...  159 us
    reduce_scatter x1, waiting for transfers between devices, body(): lax.psum_scatter(weight_part.astype(jnp.bfloat16), 'dp', scatter_dimensio...  115 us
    all_gather x1, waiting for transfers between devices, body(): gathered = lax.all_gather(normed, 'tensor', axis=0, tiled=True)  54 us
    reduce_scatter x1, waiting for transfers between devices, body(): lax.psum_scatter(partial_value.astype(jnp.bfloat16), 'tensor', scatter_di...  48.4 us
    dot_general x1, matrix products, body(): jnp.einsum('rf,nf->rn', grad_cat, cubes_serve(weight_cat), preferred_elem...  12.5 us
    dot_general x1, matrix products, body(): lax.dot_general(gathered, grad_cat, (((0,), (0,)), ((), ())), preferred_e...  12.1 us
    all_to_all x1, starting transfers between devices, cubes_serve(): jax.lax.all_to_all(jnp.stack([here_x for _ in range(jax.lax.psum(1, 'dp')...  11.6 us
  transfers between devices with their start and end apart: 4, of which 4 were waited for; matrix products, arithmetic and copies ran while one was open for 1% of the time, Pallas kernels for 0%

profile of v1, /device:TPU:8, one launch (start us, length us, event | category | flops | bytes accessed | tf_op | source)
XLA Modules:
  0.0 444.2 jit_solution(16059647206609181691)
XLA Ops:
  7.2 1.0 pad_maximum_fusion.3
  8.1 3.8 stack.2
  12.0 0.0 copy-start.2
  12.0 11.6 %all-to-all-start = ((bf16[32,64,1792]{2,1,0:T(8,128)(2,1)}), bf16[32,64,1792]{2,1,0:T(8,128)(2,1)}, u32[]{:S(2)}, u32[]{:S(2)}) async-start(bf16[32,64,1792]{2,1,0:T(8,128)(2,1)} %stack.2), calls=%async_computation | async-start | bytes 14680064 | tf_op jit(solution)/shard_map/all_to_all | solution.py:22
  23.6 0.0 reduce-scatter.3.cloned.1.call-start
  23.6 0.0 copy-done.2
  23.6 4.7 %fusion.2 = (bf16[1024,896]{1,0:T(8,128)(2,1)}, bf16[1024,896]{1,0:T(8,128)(2,1)}) fusion(bf16[1024,896]{1,0:T(8,128)(2,1)S(1)} %copy-done.2, bf16[1024,896]{1,0:T(8,128)(2,1)} %param.13, bf16[1024,896]{1,0:T(8,128)(2,1)} %param.14), kind=kLoop, calls=%fused_computation.8 | loop fusion | flops 14680064 | bytes 9175040 | tf_op jit(solution)/shard_map/convert_element_type | solution.py:42
  28.3 159.5 %all-to-all-done = bf16[32,64,1792]{2,1,0:T(8,128)(2,1)} async-done(((bf16[32,64,1792]{2,1,0:T(8,128)(2,1)}), bf16[32,64,1792]{2,1,0:T(8,128)(2,1)}, u32[]{:S(2)}, u32[]{:S(2)}) %all-to-all-start) | async-done | bytes 7340064 | tf_op jit(solution)/shard_map/all_to_all | solution.py:22
  187.7 12.5 %convolution_convert_fusion.1 = bf16[1024,2048]{1,0:T(8,128)(2,1)} fusion(bf16[2048,1792]{1,0:T(8,128)(2,1)} %bitcast, bf16[1024,896]{1,0:T(8,128)(2,1)} %get-tuple-element.4, bf16[1024,896]{1,0:T(8,128)(2,1)} %get-tuple-element.3), kind=kOutput, calls=%fused_computation.5 | convolution fusion | flops 7525629952 | bytes 15204352 | tf_op jit(solution)/shard_map/rf,nf->rn/dot_general | solution.py:47
  200.2 0.0 copy-start
  200.2 0.0 copy-start.1
  200.2 0.0 copy-start.4
  200.2 0.0 reduce-scatter.3.cloned.1.call-update
  200.3 0.0 copy-start.3
  200.3 0.0 all-gather.2.cloned.1.call-start
  200.3 1.1 copy-done
  201.4 0.1 copy-done.1
  201.6 0.0 copy-done.5
  201.6 0.3 multiply_reduce_fusion.1
  201.9 48.4 %reduce-scatter.3.cloned.1.call-done = bf16[128,2048]{1,0:T(8,128)(2,1)} async-done(((bf16[1024,2048]{1,0:T(8,128)(2,1)}), bf16[128,2048]{1,0:T(8,128)(2,1)}) %reduce-scatter.3.cloned.1.call-update) | async-done | bytes 524304 | tf_op jit(solution)/shard_map/reduce_scatter | solution.py:50
  250.3 0.0 copy-done.4
  250.3 1.5 multiply_reduce_fusion
  251.8 2.5 multiply_convert_fusion
  254.3 0.0 all-gather.2.cloned.1.call-update
  254.3 0.0 reduce-scatter.5.cloned.1.call-start
  254.4 54.0 %all-gather.2.cloned.1.call-done = bf16[1024,2048]{1,0:T(8,128)(2,1)} async-done(((bf16[128,2048]{1,0:T(8,128)(2,1)}), bf16[1024,2048]{1,0:T(8,128)(2,1)}) %all-gather.2.cloned.1.call-update) | async-done | bytes 4194320 | tf_op jit(solution)/shard_map/all_gather | solution.py:36
  308.3 0.0 copy-done.3
  308.3 12.1 %convolution_convert_fusion = bf16[2048,1792]{1,0:T(8,128)(2,1)} fusion(bf16[1024,2048]{1,0:T(8,128)(2,1)} %all-gather.2.cloned.1.call-done, bf16[1024,896]{1,0:T(8,128)(2,1)} %get-tuple-element.4, bf16[1024,896]{1,0:T(8,128)(2,1)S(1)} %copy-done.3), kind=kOutput, calls=%fused_computation | convolution fusion | flops 7527202816 | bytes 15204352 | tf_op jit(solution)/shard_map/dot_general | solution.py:60
  320.4 0.0 reduce-scatter.5.cloned.1.call-update
  320.4 115.4 %reduce-scatter.5.cloned.1.call-done = bf16[64,1792]{1,0:T(8,128)(2,1)} async-done(((bf16[2048,1792]{1,0:T(8,128)(2,1)}), bf16[64,1792]{1,0:T(8,128)(2,1)}) %reduce-scatter.5.cloned.1.call-update) | async-done | bytes 229392 | tf_op jit(solution)/shard_map/reduce_scatter | solution.py:63
  435.9 1.0 convert_multiply_fusion.4
  436.8 0.8 fusion.11
  (3 shorter events, 0.0 us)
Async XLA Ops:
  12.0 11.6 %copy-start.2 = (bf16[1024,896]{1,0:T(8,128)(2,1)S(1)}, bf16[1024,896]{1,0:T(8,128)(2,1)}, u32[]{:S(2)}) copy-start(bf16[1024,896]{1,0:T(8,128)(2,1)} %param.15) | copy-start | bytes 5505028
  12.0 175.7 %all-to-all-start = ((bf16[32,64,1792]{2,1,0:T(8,128)(2,1)}), bf16[32,64,1792]{2,1,0:T(8,128)(2,1)}, u32[]{:S(2)}, u32[]{:S(2)}) async-start(bf16[32,64,1792]{2,1,0:T(8,128)(2,1)} %stack.2), calls=%async_computation | async-start | bytes 14680064 | tf_op jit(solution)/shard_map/all_to_all | solution.py:22
  23.6 226.7 %reduce-scatter.3.cloned.1.call-start = ((), (), s32[]{:S(2)}) async-start(), calls=%async_computation.3 | async-start | bytes 4718592 | tf_op jit(solution)/shard_map/reduce_scatter | solution.py:50
  200.2 1.2 copy-start
  200.2 1.4 copy-start.1
  200.2 1.4 copy-start.5
  200.2 50.1 %copy-start.4 = (f32[2048]{0:T(1024)S(1)}, f32[2048]{0:T(1024)}, u32[]{:S(2)}) copy-start(f32[2048]{0:T(1024)} %param.12) | copy-start | bytes 24580
  200.3 108.1 %copy-start.3 = (bf16[1024,896]{1,0:T(8,128)(2,1)S(1)}, bf16[1024,896]{1,0:T(8,128)(2,1)}, u32[]{:S(2)}) copy-start(bf16[1024,896]{1,0:T(8,128)(2,1)} %get-tuple-element.3) | copy-start | bytes 5505028
  200.3 108.1 %all-gather.2.cloned.1.call-start = ((), (), s32[]{:S(2)}) async-start(), calls=%async_computation.4 | async-start | bytes 4718592 | tf_op jit(solution)/shard_map/all_gather | solution.py:36
  254.3 181.5 %reduce-scatter.5.cloned.1.call-start = ((), (), s32[]{:S(2)}) async-start(), calls=%async_computation.5 | async-start | bytes 7569408 | tf_op jit(solution)/shard_map/reduce_scatter | solution.py:63
Sparse Core Ops, SparseCore 0:
  200.4 49.8 reduce-scatter.2
  254.5 53.8 all-gather.1
  320.5 115.2 reduce-scatter.4
